TPU v7x, 32 devices: a whole 2x2x4 slice. The times are simulated.
32 devices in a mesh: sample: 4 (over z), row: 2 (over y), col: 4 (over x, core).
Axes of the slice: x: 2, y: 2, z: 4, core: 2. Of those that a mesh axis runs over, the one named last changes fastest.
Arguments:
- single: bfloat16 [2048, 384], P(('sample', 'row')), parts along dimension 0, may hold values from -16 to 16
- pair_bias: bfloat16 [64, 512, 512], P('sample', 'row', 'col'), parts along dimension 0, may hold values from -4 to 400
- token_mask: int32 [2048], P('sample'), parts along dimension 0, may hold values from 0 to 1, as said below
- norm_gain: float32 [384], replicated, may hold values from 0.25 to 1.75
- w_query: bfloat16 [384, 384], replicated, may hold values from -0.3125 to 0.3125
- query_bias: float32 [384], replicated, may hold values from -3 to 3
- w_key: bfloat16 [384, 384], replicated, may hold values from -0.3125 to 0.3125
- w_value: bfloat16 [384, 384], replicated, may hold values from -0.3125 to 0.3125
- w_gate: bfloat16 [384, 384], replicated, may hold values from -0.3125 to 0.3125
- w_out: bfloat16 [384, 384], P(None, 'col'), may hold values from -0.3125 to 0.3125
Outputs:
- updated: float32 [2048, 384], P(('sample', 'row'), 'col'), parts along dimension 0
There are 4 independent parts, one for each index of `sample`. A program takes and returns all parts, laid end to end along the dimension named above; an argument that names none is the same for every part. Nothing has to cross between parts.
Inputs may be any that keep to these rules, and one draw needn't show every extreme that they name: `token_mask`: 1 for a leading run of 64 or more tokens and 0 for every token after it.
All inputs are finite; a program needn't handle non-finite values.
Results may differ from a plain program's by a relative error of at most 0.0014.
Values may be sent and summed in bfloat16 or wider, within the bound.
No kernel may reach another device: no remote copies, remote signals or barrier semaphores. Data moves between devices by JAX's collectives and lax.ppermute only.
A program may use at most 128 MiB of HBM per device.

v0:
```python
import math
import jax
import jax.numpy as jnp
from jax import lax
from jax.sharding import PartitionSpec as P

D = 384
HEADS = 16


def layer_norm(single, norm_gain):
    values_f32 = single.astype(jnp.float32)
    row_mean = jnp.mean(values_f32, axis=1, keepdims=True)
    centered = values_f32 - row_mean
    row_var = jnp.mean(centered * centered, axis=1, keepdims=True)
    return (centered * lax.rsqrt(row_var + 1e-05) * norm_gain).astype(jnp.bfloat16)


def attend(query_rows, key_rows, value_rows, bias_block, mask_cols):
    row_count = query_rows.shape[0]
    col_count = key_rows.shape[0]
    query_heads = query_rows.reshape(row_count, HEADS, -1)
    key_heads = key_rows.reshape(col_count, HEADS, -1)
    value_heads = value_rows.reshape(col_count, HEADS, -1)
    logits = jnp.einsum("qhd,khd->hqk", query_heads, key_heads, preferred_element_type=jnp.float32)
    mask_term = (mask_cols.astype(jnp.float32) - 1.0) * 1000000.0
    logits = logits + bias_block.astype(jnp.float32) + mask_term[None, None, :]
    row_peak = jnp.max(logits, axis=2)
    exp_scores = jnp.exp(logits - row_peak[:, :, None])
    row_total = jnp.sum(exp_scores, axis=2)
    weighted = jnp.einsum(
        "hqk,khd->qhd",
        exp_scores.astype(jnp.bfloat16),
        value_heads,
        preferred_element_type=jnp.float32,
    )
    return (row_peak.T, row_total.T, weighted.reshape(row_count, -1))


def on_device(
    single, pair_bias, token_mask, norm_gain, w_query, query_bias, w_key, w_value, w_gate, w_out
):
    head_dim = D // HEADS
    inv_sqrt = 1.0 / math.sqrt(head_dim)
    tok_rows = single.shape[0]
    col_total = lax.axis_size("col")
    out_width = w_out.shape[1]
    col_pos = lax.axis_index("col")
    normed = layer_norm(single, norm_gain)
    query = (
        (jnp.dot(normed, w_query, preferred_element_type=jnp.float32) + query_bias) * inv_sqrt
    ).astype(jnp.bfloat16)
    gate_act = jax.nn.sigmoid(jnp.dot(normed, w_gate, preferred_element_type=jnp.float32))
    single_cols = lax.dynamic_slice_in_dim(single, col_pos * out_width, out_width, 1).astype(
        jnp.float32
    )
    key_local = jnp.dot(normed, w_key, preferred_element_type=jnp.float32).astype(jnp.bfloat16)
    value_local = jnp.dot(normed, w_value, preferred_element_type=jnp.float32).astype(jnp.bfloat16)
    key_all, value_all = (
        lax.all_gather(key_local, "row", axis=0, tiled=True),
        lax.all_gather(value_local, "row", axis=0, tiled=True),
    )
    sub_rows = tok_rows // col_total
    query_start = col_pos * sub_rows
    bias_panel = lax.all_to_all(pair_bias, "col", split_axis=1, concat_axis=2, tiled=True)
    key_rows, value_rows = (key_all, value_all)
    query_part = lax.dynamic_slice_in_dim(query, query_start, sub_rows, 0)
    gate_part = lax.dynamic_slice_in_dim(gate_act, query_start, sub_rows, 0)
    row_peak, row_total, weighted = attend(query_part, key_rows, value_rows, bias_panel, token_mask)
    attended = weighted / jnp.repeat(row_total, head_dim, axis=1)
    gated_part = (gate_part * attended).astype(jnp.bfloat16)
    gated_all = lax.all_gather(gated_part, "col", axis=0, tiled=True)
    result = single_cols + jnp.dot(gated_all, w_out, preferred_element_type=jnp.float32)
    return result


def solution(mesh):
    return jax.shard_map(
        on_device,
        mesh=mesh,
        in_specs=(
            P(("sample", "row"), None),
            P("sample", "row", "col"),
            P("sample"),
            P(),
            P(),
            P(),
            P(),
            P(),
            P(),
            P(None, "col"),
        ),
        out_specs=P(("sample", "row"), "col"),
        check_vma=False,
    )
```

profile of v0, /device:TPU:0, one launch (start us, length us, event | category | flops | bytes accessed | tf_op | source)
XLA Modules:
  0.0 40.1 jit_solution(15966717443112249602)
XLA Ops:
  0.0 0.0 copy-start
  0.0 0.0 copy-start.1
  0.0 0.0 copy-start.5
  0.0 2.9 %copy.31 = bf16[16,256,128]{2,0,1:T(8,128)(2,1)} copy(bf16[16,256,128]{2,1,0:T(8,128)(2,1)} %param.11) | data formatting | bytes 2097152 | tf_op args[1]
  3.0 0.0 copy-start.2
  3.0 0.0 copy-start.8
  3.0 0.0 copy-start.6
  3.0 4.4 %all-to-all-start = ((bf16[16,256,128]{2,0,1:T(8,128)(2,1)}), bf16[16,256,128]{2,0,1:T(8,128)(2,1)S(1)}, u32[]{:S(2)}, u32[]{:S(2)}) async-start(bf16[16,256,128]{2,0,1:T(8,128)(2,1)} %copy.31), calls=%async_computation | async-start | bytes 2097152 | tf_op jit(solution)/shard_map/all_to_all | solution.py:65
  7.3 0.0 copy-done.1
  7.3 0.1 convert_reduce_fusion
  7.5 0.2 fusion.7
  7.7 0.0 copy-done
  7.7 0.0 copy-done.5
  7.7 0.3 convolution_convert_fusion.1
  8.0 0.0 copy-done.2
  8.0 0.3 fusion.18
  8.4 0.0 copy-start.7
  8.4 0.0 copy-start.3
  8.4 0.0 copy-done.8
  8.4 0.3 convolution_convert_fusion
  8.8 0.0 copy-done.6
  8.8 8.5 %all_gather.9 = bf16[512,384]{1,0:T(8,128)(2,1)S(1)} all-gather(bf16[256,384]{1,0:T(8,128)(2,1)S(1)} %convolution_convert_fusion.1), channel_id=1, replica_groups=mesh['sample'=4,'row'=2,'col'=4] {'row'}, dimensions={0}, use_global_device_ids=true | all-gather | bytes 589824 | tf_op jit(solution)/shard_map/all_gather | solution.py:61
  17.3 0.2 copy.28
  17.5 0.1 copy.29
  17.6 7.3 %all_gather.10 = bf16[512,384]{1,0:T(8,128)(2,1)S(1)} all-gather(bf16[256,384]{1,0:T(8,128)(2,1)S(1)} %convolution_convert_fusion), channel_id=1, replica_groups=mesh['sample'=4,'row'=2,'col'=4] {'row'}, dimensions={0}, use_global_device_ids=true | all-gather | bytes 589824 | tf_op jit(solution)/shard_map/all_gather | solution.py:60
  24.9 0.2 copy.30
  25.1 0.1 constant_dynamic-slice_fusion
  25.3 0.1 copy.34
  25.4 0.0 copy-done.7
  25.4 0.0 copy-done.3
  25.4 1.1 %fusion.21 = f32[256,384]{1,0:T(8,128)} fusion(bf16[384,384]{1,0:T(8,128)(2,1)S(1)} %copy-done.3, bf16[256,384]{1,0:T(8,128)(2,1)S(1)} %copy-done.1, f32[384]{0:T(512)S(1)} %copy-done.5, f32[256]{0:T(256)S(1)} %add_rsqrt_fusion, f32[256]{0:T(256)S(1)} %broadcast_multiply_fusion), kind=kOutput, calls=%fused_computation.32 | convolution fusion | flops 75988992 | bytes 888320 | tf_op jit(solution)/shard_map/dot_general | solution.py:53
  26.5 0.0 all-to-all-done
  26.5 2.2 %copy.36 = f32[16,4,64,128]{3,1,2,0:T(4,128)} copy(bf16[16,4,64,128]{3,0,2,1:T(8,128)(2,1)S(1)} %bitcast.24) | data formatting | bytes 3145728 | tf_op jit(solution)/shard_map/convert_element_type | solution.py:27
  28.6 2.1 %reshape.37 = f32[16,64,512]{2,1,0:T(8,128)S(1)} reshape(f32[16,64,4,128]{3,2,1,0:T(4,128)} %bitcast.23) | data formatting | bytes 4194304 | tf_op jit(solution)/shard_map/convert_element_type | solution.py:27
  30.7 0.6 %fusion.23 = (f32[16,64]{1,0:T(8,128)S(1)}, f32[16,64,512]{2,1,0:T(8,128)S(1)}) fusion(f32[512]{0:T(512)S(1)} %add_multiply_fusion, f32[16,64,512]{2,1,0:T(8,128)S(1)} %reshape.37, bf16[64,16,24]{0,2,1:T(8,128)(2,1)S(1)} %bitcast.28, bf16[512,16,24]{0,2,1:T(8,128)(2,1)S(1)} %bitcast.25), kind=kOutput, calls=%fused_computation.33 | convolution fusion | flops 26737664 | bytes 4642816 | tf_op jit(solution)/shard_map/qhd,khd->hqk/dot_general | solution.py:25
  31.3 0.8 %fusion = f32[16,64]{1,0:T(8,128)S(1)} fusion(f32[16,64,512]{2,1,0:T(8,128)S(1)} %get-tuple-element.6, f32[16,64]{1,0:T(8,128)S(1)} %get-tuple-element.5), kind=kLoop, calls=%fused_computation.3 | loop fusion | flops 1047552 | bytes 2105344 | tf_op jit(solution)/shard_map/reduce_sum | solution.py:30
  32.1 0.0 copy-start.4
  32.1 0.5 %fusion.2 = f32[64,16,24]{0,2,1:T(8,128)S(1)} fusion(bf16[512,16,24]{0,2,1:T(8,128)(2,1)S(1)} %bitcast.26, f32[16,64,512]{2,1,0:T(8,128)S(1)} %get-tuple-element.6, f32[16,64]{1,0:T(8,128)S(1)} %get-tuple-element.5, f32[64,16]{0,1:T(8,128)S(1)} %bitcast.29), kind=kOutput, calls=%fused_computation.8 | convolution fusion | flops 26238976 | bytes 2596864 | tf_op jit(solution)/shard_map/hqk,khd->qhd/dot_general | solution.py:31
  32.6 0.1 copy.33
  32.7 0.9 %fusion.16 = bf16[64,384]{1,0:T(8,128)(2,1)S(1)} fusion(f32[64,384]{1,0:T(8,128)S(1)} %copy.33, f32[256,384]{1,0:T(8,128)} %fusion.21, s32[]{:T(128)S(6)} %select_n.8), kind=kLoop, calls=%fused_computation.26 | loop fusion | flops 122880 | bytes 245764 | tf_op jit(solution)/shard_map/convert_element_type | solution.py:71
  33.7 5.6 %all_gather.11 = bf16[256,384]{1,0:T(8,128)(2,1)S(1)} all-gather(bf16[64,384]{1,0:T(8,128)(2,1)S(1)} %fusion.16), channel_id=1, replica_groups=mesh['sample'=4,'row'=2,'col'=4] {'col'}, dimensions={0}, use_global_device_ids=true | all-gather | bytes 245760 | tf_op jit(solution)/shard_map/all_gather | solution.py:72
  39.3 0.0 copy-done.4
  39.3 0.8 %convolution_add_fusion = f32[256,96]{0,1:T(8,128)} fusion(bf16[256,384]{1,0:T(8,128)(2,1)S(1)} %all_gather.11, bf16[384,96]{0,1:T(8,128)(2,1)S(1)} %copy-done.4, bf16[256,96]{0,1:T(8,128)(2,1)S(1)} %copy.34), kind=kOutput, calls=%fused_computation.9 | convolution fusion | flops 18923520 | bytes 417792 | tf_op jit(solution)/shard_map/dot_general | solution.py:73
  (4 shorter events, 0.0 us)
Async XLA Ops:
  0.0 7.7 %copy-start = (bf16[384,384]{1,0:T(8,128)(2,1)S(1)}, bf16[384,384]{1,0:T(8,128)(2,1)}, u32[]{:S(2)}) copy-start(bf16[384,384]{1,0:T(8,128)(2,1)} %param.17) | copy-start | bytes 884740
  0.0 7.3 %copy-start.1 = (bf16[256,384]{1,0:T(8,128)(2,1)S(1)}, bf16[256,384]{1,0:T(8,128)(2,1)}, u32[]{:S(2)}) copy-start(bf16[256,384]{1,0:T(8,128)(2,1)} %param.10) | copy-start | bytes 589828
  0.0 7.7 %copy-start.5 = (f32[384]{0:T(512)S(1)}, f32[384]{0:T(512)}, u32[]{:S(2)}) copy-start(f32[384]{0:T(512)} %param.13) | copy-start | bytes 4612
  3.0 5.1 %copy-start.2 = (bf16[384,384]{1,0:T(8,128)(2,1)S(1)}, bf16[384,384]{1,0:T(8,128)(2,1)}, u32[]{:S(2)}) copy-start(bf16[384,384]{1,0:T(8,128)(2,1)} %param.14) | copy-start | bytes 884740
  3.0 5.5 %copy-start.8 = (bf16[384,384]{1,0:T(8,128)(2,1)S(1)}, bf16[384,384]{1,0:T(8,128)(2,1)}, u32[]{:S(2)}) copy-start(bf16[384,384]{1,0:T(8,128)(2,1)} %param.16) | copy-start | bytes 884740
  3.0 5.8 %copy-start.6 = (f32[384]{0:T(512)S(1)}, f32[384]{0:T(512)}, u32[]{:S(2)}) copy-start(f32[384]{0:T(512)} %param.15) | copy-start | bytes 4612
  3.0 23.5 %all-to-all-start = ((bf16[16,256,128]{2,0,1:T(8,128)(2,1)}), bf16[16,256,128]{2,0,1:T(8,128)(2,1)S(1)}, u32[]{:S(2)}, u32[]{:S(2)}) async-start(bf16[16,256,128]{2,0,1:T(8,128)(2,1)} %copy.31), calls=%async_computation | async-start | bytes 2097152 | tf_op jit(solution)/shard_map/all_to_all | solution.py:65
  8.4 17.0 %copy-start.7 = (s32[512]{0:T(512)S(1)}, s32[512]{0:T(512)}, u32[]{:S(2)}) copy-start(s32[512]{0:T(512)} %param.12) | copy-start | bytes 6148
  8.4 17.0 %copy-start.3 = (bf16[384,384]{1,0:T(8,128)(2,1)S(1)}, bf16[384,384]{1,0:T(8,128)(2,1)}, u32[]{:S(2)}) copy-start(bf16[384,384]{1,0:T(8,128)(2,1)} %param.18) | copy-start | bytes 884740
  32.1 7.2 %copy-start.4 = (bf16[384,96]{0,1:T(8,128)(2,1)S(1)}, bf16[384,96]{0,1:T(8,128)(2,1)}, u32[]{:S(2)}) copy-start(bf16[384,96]{0,1:T(8,128)(2,1)} %param.19) | copy-start | bytes 221188
where the time goes:
time: 40.4 us; the launch traced here: 40.1 us
  blocking collectives  21.4 us (53%)
  local copies, waits for them, and re-layouts  8.06 us (20%)
  starting transfers between devices  4.38 us (11%)
  matrix products  4.02 us (10%)
  other arithmetic  2.06 us (5%)
    all_gather x1, blocking collectives, on_device(): lax.all_gather(value_local, 'row', axis=0, tiled=True)  8.47 us
    all_gather x1, blocking collectives, on_device(): lax.all_gather(key_local, 'row', axis=0, tiled=True)  7.34 us
    all_gather x1, blocking collectives, on_device(): gated_all = lax.all_gather(gated_part, 'col', axis=0, tiled=True)  5.6 us
    all_to_all x1, starting transfers between devices, on_device(): lax.all_to_all(pair_bias, 'col', split_axis=1, concat_axis=2, tiled=True)  4.38 us
    convert_element_type x2, local copies, waits for them, and re-layouts, attend(): logits = logits + bias_block.astype(jnp.float32) + mask_term[None, None, :]  4.25 us
    unnamed x20, local copies, waits for them, and re-layouts  3.08 us
    dot_general x1, matrix products, on_device(): jnp.dot(normed, w_gate, preferred_element_type=jnp.float32)  1.09 us
    convert_element_type x1, other arithmetic, on_device(): gated_part = (gate_part * attended).astype(jnp.bfloat16)  0.94 us
  transfers between devices with their start and end apart: 1, of which 0 were waited for; matrix products, arithmetic and copies ran while one was open for 8% of the time, Pallas kernels for 0%

commit v1 on v0

--- a/solution.py
+++ b/solution.py
@@ -69,7 +69,12 @@
     row_peak, row_total, weighted = attend(query_part, key_rows, value_rows, bias_panel, token_mask)
     attended = weighted / jnp.repeat(row_total, head_dim, axis=1)
     gated_part = (gate_part * attended).astype(jnp.bfloat16)
-    gated_all = lax.all_gather(gated_part, "col", axis=0, tiled=True)
+    ring = [gated_part]
+    for hop in range(3):
+        ring.append(lax.ppermute(ring[-1], "col", [(dev, (dev + 1) % 4) for dev in range(4)]))
+    gated_all = jnp.roll(
+        jnp.concatenate(ring[::-1], axis=0), (lax.axis_index("col") + 1) * ring[0].shape[0], axis=0
+    )
     result = single_cols + jnp.dot(gated_all, w_out, preferred_element_type=jnp.float32)
     return result
 

time: 40.4 us -> 46.2 us (1.14)
  waiting for transfers between devices: 0.01 us -> 10.3 us
  blocking collectives: 21.4 us -> 15.8 us
  matrix products: 4.02 us -> 4.97 us
    ppermute x0 -> x3, waiting for transfers between devices: none -> 10.3 us  [on_device(): lax.ppermute(ring[-1], 'col', [(dev, (dev + 1) % 4) for dev in range(4)])]
    all_gather x1 -> x0, blocking collectives: 5.6 us -> none  [on_device(): gated_all = lax.all_gather(gated_part, 'col', axis=0, tiled=True)]
    dot_general x1, matrix products: 0.34 us -> 1.29 us  [on_device(): jnp.dot(normed, w_key, preferred_element_type=jnp.float32)]
    unnamed x20 -> x25, local copies, waits for them, and re-layouts: 3.08 us -> 3.14 us
  transfers between devices with their start and end apart: 1 -> 4, of which waited for: 0 -> 3; matrix products, arithmetic and copies ran while one was open for 8% -> 9% of each run, Pallas kernels for 0% -> 0%
where the time goes in v1:
time: 46.2 us; the launch traced here: 45.9 us
  blocking collectives  15.8 us (34%)
  waiting for transfers between devices  10.3 us (22%)
  local copies, waits for them, and re-layouts  8.11 us (18%)
  matrix products  4.97 us (11%)
  starting transfers between devices  4.44 us (10%)
  other arithmetic  2.06 us (4%)
    ppermute x3, waiting for transfers between devices, on_device(): lax.ppermute(ring[-1], 'col', [(dev, (dev + 1) % 4) for dev in range(4)])  10.3 us
    all_gather x1, blocking collectives, on_device(): lax.all_gather(value_local, 'row', axis=0, tiled=True)  8.48 us
    all_gather x1, blocking collectives, on_device(): lax.all_gather(key_local, 'row', axis=0, tiled=True)  7.34 us
    all_to_all x1, starting transfers between devices, on_device(): lax.all_to_all(pair_bias, 'col', split_axis=1, concat_axis=2, tiled=True)  4.38 us
    convert_element_type x2, local copies, waits for them, and re-layouts, attend(): logits = logits + bias_block.astype(jnp.float32) + mask_term[None, None, :]  4.24 us
    unnamed x25, local copies, waits for them, and re-layouts  3.14 us
    dot_general x1, matrix products, on_device(): jnp.dot(normed, w_key, preferred_element_type=jnp.float32)  1.29 us
    dot_general x1, matrix products, on_device(): jnp.dot(normed, w_gate, preferred_element_type=jnp.float32)  1.08 us
  transfers between devices with their start and end apart: 4, of which 3 were waited for; matrix products, arithmetic and copies ran while one was open for 9% of the time, Pallas kernels for 0%

profile of v1, /device:TPU:0, one launch (start us, length us, event | category | flops | bytes accessed | tf_op | source)
XLA Modules:
  0.0 45.9 jit_solution(15039085532797511887)
XLA Ops:
  0.0 0.0 copy-start
  0.0 0.0 copy-start.1
  0.0 0.0 copy-start.5
  0.0 2.9 %copy.26 = bf16[16,256,128]{2,0,1:T(8,128)(2,1)} copy(bf16[16,256,128]{2,1,0:T(8,128)(2,1)} %param.11) | data formatting | bytes 2097152 | tf_op args[1]
  2.9 0.0 copy-start.2
  2.9 4.4 %all-to-all-start = ((bf16[16,256,128]{2,0,1:T(8,128)(2,1)}), bf16[16,256,128]{2,0,1:T(8,128)(2,1)S(1)}, u32[]{:S(2)}, u32[]{:S(2)}) async-start(bf16[16,256,128]{2,0,1:T(8,128)(2,1)} %copy.26), calls=%async_computation | async-start | bytes 2097152 | tf_op jit(solution)/shard_map/all_to_all | solution.py:65
  7.3 0.0 copy-start.6
  7.3 0.0 copy-done.1
  7.3 0.1 convert_reduce_fusion
  7.5 0.2 fusion.7
  7.7 0.0 copy-done
  7.7 0.0 copy-done.5
  7.7 0.3 convolution_convert_fusion.1
  8.0 8.5 %all_gather.6 = bf16[512,384]{1,0:T(8,128)(2,1)S(1)} all-gather(bf16[256,384]{1,0:T(8,128)(2,1)S(1)} %convolution_convert_fusion.1), channel_id=1, replica_groups=mesh['sample'=4,'row'=2,'col'=4] {'row'}, dimensions={0}, use_global_device_ids=true | all-gather | bytes 589824 | tf_op jit(solution)/shard_map/all_gather | solution.py:61
  16.5 0.0 copy-start.7
  16.5 0.0 copy-start.3
  16.5 0.2 copy.23
  16.7 0.0 copy-done.2
  16.7 0.3 fusion.20
  17.0 0.0 copy-done.6
  17.1 0.1 copy.24
  17.2 1.3 %convolution_convert_fusion = bf16[256,384]{1,0:T(8,128)(2,1)S(1)} fusion(bf16[384,384]{1,0:T(8,128)(2,1)} %param.16, bf16[256,384]{1,0:T(8,128)(2,1)S(1)} %copy-done.1, f32[384]{0:T(512)S(1)} %copy-done.5, f32[256]{0:T(256)S(1)} %add_rsqrt_fusion, f32[256]{0:T(256)S(1)} %broadcast_multiply_fusion), kind=kOutput, calls=%fused_computation.5 | convolution fusion | flops 76087296 | bytes 691712 | tf_op jit(solution)/shard_map/dot_general | solution.py:57
  18.5 7.3 %all_gather.7 = bf16[512,384]{1,0:T(8,128)(2,1)S(1)} all-gather(bf16[256,384]{1,0:T(8,128)(2,1)S(1)} %convolution_convert_fusion), channel_id=1, replica_groups=mesh['sample'=4,'row'=2,'col'=4] {'row'}, dimensions={0}, use_global_device_ids=true | all-gather | bytes 589824 | tf_op jit(solution)/shard_map/all_gather | solution.py:60
  25.9 0.2 copy.25
  26.0 0.0 copy-done.7
  26.1 0.0 copy-done.3
  26.1 1.1 %fusion.23 = f32[256,384]{1,0:T(8,128)} fusion(bf16[384,384]{1,0:T(8,128)(2,1)S(1)} %copy-done.3, bf16[256,384]{1,0:T(8,128)(2,1)S(1)} %copy-done.1, f32[384]{0:T(512)S(1)} %copy-done.5, f32[256]{0:T(256)S(1)} %add_rsqrt_fusion, f32[256]{0:T(256)S(1)} %broadcast_multiply_fusion), kind=kOutput, calls=%fused_computation.42 | convolution fusion | flops 75988992 | bytes 888320 | tf_op jit(solution)/shard_map/dot_general | solution.py:53
  27.2 0.0 all-to-all-done
  27.2 2.1 %copy.31 = f32[16,4,64,128]{3,1,2,0:T(4,128)} copy(bf16[16,4,64,128]{3,0,2,1:T(8,128)(2,1)S(1)} %bitcast.23) | data formatting | bytes 3145728 | tf_op jit(solution)/shard_map/convert_element_type | solution.py:27
  29.3 2.1 %reshape.37 = f32[16,64,512]{2,1,0:T(8,128)S(1)} reshape(f32[16,64,4,128]{3,2,1,0:T(4,128)} %bitcast.22) | data formatting | bytes 4194304 | tf_op jit(solution)/shard_map/convert_element_type | solution.py:27
  31.4 0.6 %fusion.25 = (f32[16,64]{1,0:T(8,128)S(1)}, f32[16,64,512]{2,1,0:T(8,128)S(1)}) fusion(f32[512]{0:T(512)S(1)} %add_multiply_fusion, f32[16,64,512]{2,1,0:T(8,128)S(1)} %reshape.37, bf16[64,16,24]{0,2,1:T(8,128)(2,1)S(1)} %bitcast.27, bf16[512,16,24]{0,2,1:T(8,128)(2,1)S(1)} %bitcast.24), kind=kOutput, calls=%fused_computation.43 | convolution fusion | flops 26737664 | bytes 4642816 | tf_op jit(solution)/shard_map/qhd,khd->hqk/dot_general | solution.py:25
  32.0 0.8 %fusion = f32[16,64]{1,0:T(8,128)S(1)} fusion(f32[16,64,512]{2,1,0:T(8,128)S(1)} %get-tuple-element.6, f32[16,64]{1,0:T(8,128)S(1)} %get-tuple-element.5), kind=kLoop, calls=%fused_computation.3 | loop fusion | flops 1047552 | bytes 2105344 | tf_op jit(solution)/shard_map/reduce_sum | solution.py:30
  32.8 0.0 copy-start.4
  32.8 0.5 %fusion.2 = f32[64,16,24]{0,2,1:T(8,128)S(1)} fusion(bf16[512,16,24]{0,2,1:T(8,128)(2,1)S(1)} %bitcast.25, f32[16,64,512]{2,1,0:T(8,128)S(1)} %get-tuple-element.6, f32[16,64]{1,0:T(8,128)S(1)} %get-tuple-element.5, f32[64,16]{0,1:T(8,128)S(1)} %bitcast.28), kind=kOutput, calls=%fused_computation.8 | convolution fusion | flops 26238976 | bytes 2596864 | tf_op jit(solution)/shard_map/hqk,khd->qhd/dot_general | solution.py:31
  33.3 0.1 copy.28
  33.4 0.9 %fusion.17 = bf16[64,384]{1,0:T(8,128)(2,1)S(1)} fusion(f32[64,384]{1,0:T(8,128)S(1)} %copy.28, f32[256,384]{1,0:T(8,128)} %fusion.23, s32[]{:T(128)S(6)} %select_n.21), kind=kLoop, calls=%fused_computation.27 | loop fusion | flops 122880 | bytes 245764 | tf_op jit(solution)/shard_map/convert_element_type | solution.py:71
  34.3 0.1 collective-permute-start
  34.4 3.5 %collective-permute-done = bf16[64,384]{1,0:T(8,128)(2,1)S(1)} collective-permute-done((bf16[64,384]{1,0:T(8,128)(2,1)S(1)}, bf16[64,384]{1,0:T(8,128)(2,1)S(1)}, u32[]{:S(2)}, u32[]{:S(2)}) %collective-permute-start) | collective-permute-done | bytes 49184 | tf_op jit(solution)/shard_map/ppermute | solution.py:74
  37.9 0.0 collective-permute-start.1
  37.9 3.5 %collective-permute-done.1 = bf16[64,384]{1,0:T(8,128)(2,1)S(1)} collective-permute-done((bf16[64,384]{1,0:T(8,128)(2,1)S(1)}, bf16[64,384]{1,0:T(8,128)(2,1)S(1)}, u32[]{:S(2)}, u32[]{:S(2)}) %collective-permute-start.1) | collective-permute-done | bytes 49184 | tf_op jit(solution)/shard_map/ppermute | solution.py:74
  41.4 0.0 collective-permute-start.2
  41.4 0.1 constant_dynamic-slice_fusion
  41.5 0.1 copy.29
  41.7 3.3 %collective-permute-done.2 = bf16[64,384]{1,0:T(8,128)(2,1)S(1)} collective-permute-done((bf16[64,384]{1,0:T(8,128)(2,1)S(1)}, bf16[64,384]{1,0:T(8,128)(2,1)S(1)}, u32[]{:S(2)}, u32[]{:S(2)}) %collective-permute-start.2) | collective-permute-done | bytes 49184 | tf_op jit(solution)/shard_map/ppermute | solution.py:74
  45.1 0.0 copy-done.4
  45.1 0.9 %convolution_add_fusion = f32[256,96]{0,1:T(8,128)} fusion(bf16[384,96]{0,1:T(8,128)(2,1)S(1)} %copy-done.4, bf16[512,384]{1,0:T(8,128)(2,1)S(1)} %constant_dynamic-update-slice_fusion, s32[]{:T(128)S(6)} %select_n.23, bf16[256,96]{0,1:T(8,128)(2,1)S(1)} %copy.29), kind=kOutput, calls=%fused_computation.9 | convolution fusion | flops 18923520 | bytes 417796 | tf_op jit(solution)/shard_map/dot_general | solution.py:78
  (12 shorter events, 0.1 us)
Async XLA Ops:
  0.0 7.7 %copy-start = (bf16[384,384]{1,0:T(8,128)(2,1)S(1)}, bf16[384,384]{1,0:T(8,128)(2,1)}, u32[]{:S(2)}) copy-start(bf16[384,384]{1,0:T(8,128)(2,1)} %param.17) | copy-start | bytes 884740
  0.0 7.3 %copy-start.1 = (bf16[256,384]{1,0:T(8,128)(2,1)S(1)}, bf16[256,384]{1,0:T(8,128)(2,1)}, u32[]{:S(2)}) copy-start(bf16[256,384]{1,0:T(8,128)(2,1)} %param.10) | copy-start | bytes 589828
  0.0 7.7 %copy-start.5 = (f32[384]{0:T(512)S(1)}, f32[384]{0:T(512)}, u32[]{:S(2)}) copy-start(f32[384]{0:T(512)} %param.13) | copy-start | bytes 4612
  2.9 13.8 %copy-start.2 = (bf16[384,384]{1,0:T(8,128)(2,1)S(1)}, bf16[384,384]{1,0:T(8,128)(2,1)}, u32[]{:S(2)}) copy-start(bf16[384,384]{1,0:T(8,128)(2,1)} %param.14) | copy-start | bytes 884740
  2.9 24.2 %all-to-all-start = ((bf16[16,256,128]{2,0,1:T(8,128)(2,1)}), bf16[16,256,128]{2,0,1:T(8,128)(2,1)S(1)}, u32[]{:S(2)}, u32[]{:S(2)}) async-start(bf16[16,256,128]{2,0,1:T(8,128)(2,1)} %copy.26), calls=%async_computation | async-start | bytes 2097152 | tf_op jit(solution)/shard_map/all_to_all | solution.py:65
  7.3 9.7 %copy-start.6 = (f32[384]{0:T(512)S(1)}, f32[384]{0:T(512)}, u32[]{:S(2)}) copy-start(f32[384]{0:T(512)} %param.15) | copy-start | bytes 4612
  16.5 9.6 %copy-start.7 = (s32[512]{0:T(512)S(1)}, s32[512]{0:T(512)}, u32[]{:S(2)}) copy-start(s32[512]{0:T(512)} %param.12) | copy-start | bytes 6148
  16.5 9.6 %copy-start.3 = (bf16[384,384]{1,0:T(8,128)(2,1)S(1)}, bf16[384,384]{1,0:T(8,128)(2,1)}, u32[]{:S(2)}) copy-start(bf16[384,384]{1,0:T(8,128)(2,1)} %param.18) | copy-start | bytes 884740
  32.8 12.3 %copy-start.4 = (bf16[384,96]{0,1:T(8,128)(2,1)S(1)}, bf16[384,96]{0,1:T(8,128)(2,1)}, u32[]{:S(2)}) copy-start(bf16[384,96]{0,1:T(8,128)(2,1)} %param.19) | copy-start | bytes 221188
  34.3 3.6 %collective-permute-start = (bf16[64,384]{1,0:T(8,128)(2,1)S(1)}, bf16[64,384]{1,0:T(8,128)(2,1)S(1)}, u32[]{:S(2)}, u32[]{:S(2)}) collective-permute-start(bf16[64,384]{1,0:T(8,128)(2,1)S(1)} %fusion.17), channel_id=1, source_target_pairs={{0,1},{1,2},{2,3},{3,0},{4,5},{5,6},{6,7},{7,4},{8,9},{9,10},{10,1... | collective-permute-start | bytes 147464 | tf_op jit(solution)/shard_map/ppermute | solution.py:74
  37.9 3.5 %collective-permute-start.1 = (bf16[64,384]{1,0:T(8,128)(2,1)S(1)}, bf16[64,384]{1,0:T(8,128)(2,1)S(1)}, u32[]{:S(2)}, u32[]{:S(2)}) collective-permute-start(bf16[64,384]{1,0:T(8,128)(2,1)S(1)} %collective-permute-done), channel_id=1, source_target_pairs={{0,1},{1,2},{2,3},{3,0},{4,5},{5,6},{6,7},{7,4},{8,9},{9,10},{10,1... | collective-permute-start | bytes 147464 | tf_op jit(solution)/shard_map/ppermute | solution.py:74
  41.4 3.5 %collective-permute-start.2 = (bf16[64,384]{1,0:T(8,128)(2,1)S(1)}, bf16[64,384]{1,0:T(8,128)(2,1)S(1)}, u32[]{:S(2)}, u32[]{:S(2)}) collective-permute-start(bf16[64,384]{1,0:T(8,128)(2,1)S(1)} %collective-permute-done.1), channel_id=1, source_target_pairs={{0,1},{1,2},{2,3},{3,0},{4,5},{5,6},{6,7},{7,4},{8,9},{9,10},{10,1... | collective-permute-start | bytes 147464 | tf_op jit(solution)/shard_map/ppermute | solution.py:74
